TPU v7x, 128 devices: a whole 4x4x4 slice. The times are simulated.
128 devices in a mesh: rep: 16 (over x, y_lo, core), shard: 8 (over y_hi, z).
Axes of the slice: x: 4, y: 4 (y_hi: 2, y_lo: 2; y = y_hi * 2 + y_lo), z: 4, core: 2. Of those that a mesh axis runs over, the one named last changes fastest.
Arguments:
- x_in: bfloat16 [40960, 1024], P(('rep', 'shard')), may hold values from -6 to 6
- cotangent: float32 [40960, 1024], P(('rep', 'shard')), may hold values from -24 to 24
- ln1_gain: bfloat16 [1024], P('shard'), may hold values from 0.5 to 1.5
- ln1_bias: bfloat16 [1024], P('shard'), may hold values from -3 to 3
- w_qkv: bfloat16 [1024, 3072], P('shard'), may hold values from -8 to 8
- q_bias: bfloat16 [1024], P('shard'), may hold values from -3 to 3
- v_bias: bfloat16 [1024], P('shard'), may hold values from -3 to 3
- w_attn_out: bfloat16 [1024, 1024], P('shard'), may hold values from -0.75 to 0.75
- out_bias: bfloat16 [1024], P('shard'), may hold values from -3 to 3
- ln2_gain: bfloat16 [1024], P('shard'), may hold values from 0.5 to 1.5
- ln2_bias: bfloat16 [1024], P('shard'), may hold values from -3 to 3
- w_up: bfloat16 [1024, 4096], P('shard'), may hold values from -0.1875 to 0.1875
- up_bias: bfloat16 [4096], P('shard'), may hold values from -3 to 3
- w_down: bfloat16 [4096, 1024], P('shard'), may hold values from -0.09375 to 0.09375
- down_bias: bfloat16 [1024], P('shard'), may hold values from -3 to 3
Outputs:
- block_out: bfloat16 [40960, 1024], P(('rep', 'shard'))
- input_grad: float32 [40960, 1024], P(('rep', 'shard'))
- grad_ln1_gain: float32 [1024], P('shard')
- grad_ln1_bias: float32 [1024], P('shard')
- grad_w_qkv: float32 [1024, 3072], P('shard')
- grad_q_bias: float32 [1024], P('shard')
- grad_v_bias: float32 [1024], P('shard')
- grad_w_attn_out: float32 [1024, 1024], P('shard')
- grad_out_bias: float32 [1024], P('shard')
- grad_ln2_gain: float32 [1024], P('shard')
- grad_ln2_bias: float32 [1024], P('shard')
- grad_w_up: float32 [1024, 4096], P('shard')
- grad_up_bias: float32 [4096], P('shard')
- grad_w_down: float32 [4096, 1024], P('shard')
- grad_down_bias: float32 [1024], P('shard')
All inputs are finite; a program needn't handle non-finite values.
Results may differ from a plain program's by a relative error of at most 0.023.
Values may be sent and summed in bfloat16 or wider, within the bound.
A program may use at most 192 MiB of HBM per device.

v0:
```python
import math
import jax
import jax.numpy as jnp
from jax import lax
from jax.sharding import PartitionSpec as P

HEADS = 16
HEAD_DIM = 64
SEQ = 320
eps_norm = 1e-05
sqrt_two_pi = math.sqrt(2.0 / math.pi)
cubic_coef = 0.044715


def gelu_value(up_projected):
    inner = sqrt_two_pi * (up_projected + cubic_coef * up_projected * up_projected * up_projected)
    return 0.5 * up_projected * (1.0 + jnp.tanh(inner))


def gelu_slope(up_projected):
    tanh_val = jnp.tanh(
        sqrt_two_pi * (up_projected + cubic_coef * up_projected * up_projected * up_projected)
    )
    return 0.5 * (1.0 + tanh_val) + 0.5 * up_projected * (
        1.0 - tanh_val * tanh_val
    ) * sqrt_two_pi * (1.0 + 3.0 * cubic_coef * up_projected * up_projected)


def layer_normalize(rows_in, gain_vec, bias_vec):
    center = rows_in - jnp.mean(rows_in, axis=-1, keepdims=True)
    inv_std = lax.rsqrt(jnp.mean(center * center, axis=-1, keepdims=True) + eps_norm)
    x_hat = center * inv_std
    return (x_hat * gain_vec.astype(jnp.float32) + bias_vec.astype(jnp.float32), x_hat, inv_std)


def layer_normalize_backward(d_normed, x_hat, inv_std):
    return inv_std * (
        d_normed
        - jnp.mean(d_normed, axis=-1, keepdims=True)
        - x_hat * jnp.mean(d_normed * x_hat, axis=-1, keepdims=True)
    )


def split_heads(rows_in):
    return rows_in.reshape(rows_in.shape[0] // SEQ, SEQ, HEADS, HEAD_DIM)


def merge_heads(heads_in):
    return heads_in.reshape(-1, HEADS * HEAD_DIM)


def alibi_bias():
    positions = jnp.arange(SEQ)
    distance = (positions[:, None] - positions[None, :]).astype(jnp.float32)
    head_ids = jnp.arange(HEADS).astype(jnp.float32)
    slopes = jnp.exp2(-8.0 * (head_ids + 1.0) / HEADS)
    offsets = -slopes[:, None, None] * distance[None, :, :]
    return jnp.where(distance[None, :, :] >= 0.0, offsets, -jnp.inf)


def attn_scores(query_heads, key_heads):
    scores = jnp.einsum(
        "bqhd,bkhd->bhqk", query_heads, key_heads, preferred_element_type=jnp.float32
    )
    return scores * HEAD_DIM ** (-0.5) + alibi_bias()[None]


def layer_forward(x_in, params):
    (
        first_norm_gain,
        first_norm_bias,
        w_qkv,
        q_bias,
        v_bias,
        w_attn_out,
        out_bias,
        second_norm_gain,
        second_norm_bias,
        w_up,
        up_bias,
        w_down,
        down_bias,
    ) = params
    model_width = x_in.shape[1]
    residual_input = x_in.astype(jnp.float32)
    first_normalized, first_centered_scaled, first_inverse_scale = layer_normalize(
        residual_input, first_norm_gain, first_norm_bias
    )
    first_activation = first_normalized.astype(jnp.bfloat16)
    united_proj = jnp.dot(first_activation, w_qkv, preferred_element_type=jnp.float32)
    query_block = (united_proj[:, :model_width] + q_bias.astype(jnp.float32)).astype(jnp.bfloat16)
    key_block = united_proj[:, model_width : 2 * model_width].astype(jnp.bfloat16)
    value_block = (united_proj[:, 2 * model_width :] + v_bias.astype(jnp.float32)).astype(
        jnp.bfloat16
    )
    scores = attn_scores(split_heads(query_block), split_heads(key_block))
    maximum = jnp.max(scores, axis=-1, keepdims=True)
    log_normalizer = maximum + jnp.log(jnp.sum(jnp.exp(scores - maximum), axis=-1, keepdims=True))
    probab = jnp.exp(scores - log_normalizer).astype(jnp.bfloat16)
    attended_context = merge_heads(
        jnp.einsum(
            "bhqk,bkhd->bqhd", probab, split_heads(value_block), preferred_element_type=jnp.float32
        )
    ).astype(jnp.bfloat16)
    residual_middle = (
        residual_input
        + jnp.dot(attended_context, w_attn_out, preferred_element_type=jnp.float32)
        + out_bias.astype(jnp.float32)
    )
    second_normalized, second_centered_scaled, second_inverse_scale = layer_normalize(
        residual_middle, second_norm_gain, second_norm_bias
    )
    second_activation = second_normalized.astype(jnp.bfloat16)
    up_projected = jnp.dot(
        second_activation, w_up, preferred_element_type=jnp.float32
    ) + up_bias.astype(jnp.float32)
    hidden_activations = gelu_value(up_projected).astype(jnp.bfloat16)
    block_out = (
        residual_middle
        + jnp.dot(hidden_activations, w_down, preferred_element_type=jnp.float32)
        + down_bias.astype(jnp.float32)
    ).astype(jnp.bfloat16)
    saved_state = (
        first_centered_scaled,
        first_inverse_scale,
        first_activation,
        query_block,
        key_block,
        value_block,
        log_normalizer,
        attended_context,
        second_centered_scaled,
        second_inverse_scale,
        second_activation,
        up_projected,
        hidden_activations,
    )
    return (block_out, saved_state)


def layer_backward(cotangent, saved_state, params):
    (
        first_norm_gain,
        first_norm_bias,
        w_qkv,
        q_bias,
        v_bias,
        w_attn_out,
        out_bias,
        second_norm_gain,
        second_norm_bias,
        w_up,
        up_bias,
        w_down,
        down_bias,
    ) = params
    (
        first_centered_scaled,
        first_inverse_scale,
        first_activation,
        query_block,
        key_block,
        value_block,
        log_normalizer,
        attended_context,
        second_centered_scaled,
        second_inverse_scale,
        second_activation,
        up_projected,
        hidden_activations,
    ) = saved_state
    cot_b = cotangent.astype(jnp.bfloat16)
    g_down_bias = jnp.sum(cotangent, axis=0)
    g_w_down = jnp.dot(hidden_activations.T, cot_b, preferred_element_type=jnp.float32)
    d_up = jnp.dot(cot_b, w_down.T, preferred_element_type=jnp.float32) * gelu_slope(up_projected)
    g_up_bias = jnp.sum(d_up, axis=0)
    d_up_b = d_up.astype(jnp.bfloat16)
    g_w_up = jnp.dot(second_activation.T, d_up_b, preferred_element_type=jnp.float32)
    second_activation_grad = jnp.dot(d_up_b, w_up.T, preferred_element_type=jnp.float32)
    second_gain_grad = jnp.sum(second_activation_grad * second_centered_scaled, axis=0)
    g_bias_two = jnp.sum(second_activation_grad, axis=0)
    middle_residual_grad = cotangent + layer_normalize_backward(
        second_activation_grad * second_norm_gain.astype(jnp.float32),
        second_centered_scaled,
        second_inverse_scale,
    )
    g_out_bias = jnp.sum(middle_residual_grad, axis=0)
    d_mid_b = middle_residual_grad.astype(jnp.bfloat16)
    g_w_attn_out = jnp.dot(attended_context.T, d_mid_b, preferred_element_type=jnp.float32)
    d_context = jnp.dot(d_mid_b, w_attn_out.T, preferred_element_type=jnp.float32).astype(
        jnp.bfloat16
    )
    query_heads = split_heads(query_block)
    key_heads = split_heads(key_block)
    scores = attn_scores(query_heads, key_heads)
    probab = jnp.exp(scores - log_normalizer)
    probab_b = probab.astype(jnp.bfloat16)
    ctx_heads = split_heads(d_context)
    d_value = merge_heads(
        jnp.einsum("bhqk,bqhd->bkhd", probab_b, ctx_heads, preferred_element_type=jnp.float32)
    )
    d_prob = jnp.einsum(
        "bqhd,bkhd->bhqk", ctx_heads, split_heads(value_block), preferred_element_type=jnp.float32
    )
    d_score = probab * (d_prob - jnp.sum(probab * d_prob, axis=-1, keepdims=True))
    d_score_b = d_score.astype(jnp.bfloat16)
    d_query = merge_heads(
        jnp.einsum("bhqk,bkhd->bqhd", d_score_b, key_heads, preferred_element_type=jnp.float32)
    ) * HEAD_DIM ** (-0.5)
    d_key = merge_heads(
        jnp.einsum("bhqk,bqhd->bkhd", d_score_b, query_heads, preferred_element_type=jnp.float32)
    ) * HEAD_DIM ** (-0.5)
    g_q_bias = jnp.sum(d_query, axis=0)
    g_v_bias = jnp.sum(d_value, axis=0)
    d_united = jnp.concatenate([d_query, d_key, d_value], axis=1).astype(jnp.bfloat16)
    g_w_qkv = jnp.dot(first_activation.T, d_united, preferred_element_type=jnp.float32)
    first_activation_grad = jnp.dot(d_united, w_qkv.T, preferred_element_type=jnp.float32)
    first_gain_grad = jnp.sum(first_activation_grad * first_centered_scaled, axis=0)
    g_bias_one = jnp.sum(first_activation_grad, axis=0)
    layer_input_grad = middle_residual_grad + layer_normalize_backward(
        first_activation_grad * first_norm_gain.astype(jnp.float32),
        first_centered_scaled,
        first_inverse_scale,
    )
    grads = (
        first_gain_grad,
        g_bias_one,
        g_w_qkv,
        g_q_bias,
        g_v_bias,
        g_w_attn_out,
        g_out_bias,
        second_gain_grad,
        g_bias_two,
        g_w_up,
        g_up_bias,
        g_w_down,
        g_down_bias,
    )
    return (layer_input_grad, grads)


def on_device(
    x_in,
    cotangent,
    ln1_gain,
    ln1_bias,
    w_qkv,
    q_bias,
    v_bias,
    w_attn_out,
    out_bias,
    ln2_gain,
    ln2_bias,
    w_up,
    up_bias,
    w_down,
    down_bias,
):
    gathered = (
        lax.all_gather(ln1_gain, "shard", axis=0, tiled=True),
        lax.all_gather(ln1_bias, "shard", axis=0, tiled=True),
        lax.all_gather(w_qkv, "shard", axis=0, tiled=True),
        lax.all_gather(q_bias, "shard", axis=0, tiled=True),
        lax.all_gather(v_bias, "shard", axis=0, tiled=True),
        lax.all_gather(w_attn_out, "shard", axis=0, tiled=True),
        lax.all_gather(out_bias, "shard", axis=0, tiled=True),
        lax.all_gather(ln2_gain, "shard", axis=0, tiled=True),
        lax.all_gather(ln2_bias, "shard", axis=0, tiled=True),
        lax.all_gather(w_up, "shard", axis=0, tiled=True),
        lax.all_gather(up_bias, "shard", axis=0, tiled=True),
        lax.all_gather(w_down, "shard", axis=0, tiled=True),
        lax.all_gather(down_bias, "shard", axis=0, tiled=True),
    )
    block_out, saved_state = layer_forward(x_in, gathered)
    again = (
        lax.all_gather(ln1_gain, "shard", axis=0, tiled=True),
        lax.all_gather(ln1_bias, "shard", axis=0, tiled=True),
        lax.all_gather(w_qkv, "shard", axis=0, tiled=True),
        lax.all_gather(q_bias, "shard", axis=0, tiled=True),
        lax.all_gather(v_bias, "shard", axis=0, tiled=True),
        lax.all_gather(w_attn_out, "shard", axis=0, tiled=True),
        lax.all_gather(out_bias, "shard", axis=0, tiled=True),
        lax.all_gather(ln2_gain, "shard", axis=0, tiled=True),
        lax.all_gather(ln2_bias, "shard", axis=0, tiled=True),
        lax.all_gather(w_up, "shard", axis=0, tiled=True),
        lax.all_gather(up_bias, "shard", axis=0, tiled=True),
        lax.all_gather(w_down, "shard", axis=0, tiled=True),
        lax.all_gather(down_bias, "shard", axis=0, tiled=True),
    )
    layer_input_grad, grads = layer_backward(cotangent, saved_state, again)
    shares = (
        lax.psum_scatter(
            grads[0].astype(jnp.bfloat16), "shard", scatter_dimension=0, tiled=True
        ).astype(jnp.float32),
        lax.psum_scatter(
            grads[1].astype(jnp.bfloat16), "shard", scatter_dimension=0, tiled=True
        ).astype(jnp.float32),
        lax.psum_scatter(
            grads[2].astype(jnp.bfloat16), "shard", scatter_dimension=0, tiled=True
        ).astype(jnp.float32),
        lax.psum_scatter(
            grads[3].astype(jnp.bfloat16), "shard", scatter_dimension=0, tiled=True
        ).astype(jnp.float32),
        lax.psum_scatter(
            grads[4].astype(jnp.bfloat16), "shard", scatter_dimension=0, tiled=True
        ).astype(jnp.float32),
        lax.psum_scatter(
            grads[5].astype(jnp.bfloat16), "shard", scatter_dimension=0, tiled=True
        ).astype(jnp.float32),
        lax.psum_scatter(
            grads[6].astype(jnp.bfloat16), "shard", scatter_dimension=0, tiled=True
        ).astype(jnp.float32),
        lax.psum_scatter(
            grads[7].astype(jnp.bfloat16), "shard", scatter_dimension=0, tiled=True
        ).astype(jnp.float32),
        lax.psum_scatter(
            grads[8].astype(jnp.bfloat16), "shard", scatter_dimension=0, tiled=True
        ).astype(jnp.float32),
        lax.psum_scatter(
            grads[9].astype(jnp.bfloat16), "shard", scatter_dimension=0, tiled=True
        ).astype(jnp.float32),
        lax.psum_scatter(
            grads[10].astype(jnp.bfloat16), "shard", scatter_dimension=0, tiled=True
        ).astype(jnp.float32),
        lax.psum_scatter(
            grads[11].astype(jnp.bfloat16), "shard", scatter_dimension=0, tiled=True
        ).astype(jnp.float32),
        lax.psum_scatter(
            grads[12].astype(jnp.bfloat16), "shard", scatter_dimension=0, tiled=True
        ).astype(jnp.float32),
    )
    totals = (
        lax.psum(shares[0].astype(jnp.bfloat16), "rep").astype(jnp.float32),
        lax.psum(shares[1].astype(jnp.bfloat16), "rep").astype(jnp.float32),
        lax.psum(shares[2].astype(jnp.bfloat16), "rep").astype(jnp.float32),
        lax.psum(shares[3].astype(jnp.bfloat16), "rep").astype(jnp.float32),
        lax.psum(shares[4].astype(jnp.bfloat16), "rep").astype(jnp.float32),
        lax.psum(shares[5].astype(jnp.bfloat16), "rep").astype(jnp.float32),
        lax.psum(shares[6].astype(jnp.bfloat16), "rep").astype(jnp.float32),
        lax.psum(shares[7].astype(jnp.bfloat16), "rep").astype(jnp.float32),
        lax.psum(shares[8].astype(jnp.bfloat16), "rep").astype(jnp.float32),
        lax.psum(shares[9].astype(jnp.bfloat16), "rep").astype(jnp.float32),
        lax.psum(shares[10].astype(jnp.bfloat16), "rep").astype(jnp.float32),
        lax.psum(shares[11].astype(jnp.bfloat16), "rep").astype(jnp.float32),
        lax.psum(shares[12].astype(jnp.bfloat16), "rep").astype(jnp.float32),
    )
    seq_count = x_in.shape[0] // SEQ * lax.axis_size("rep") * lax.axis_size("shard")
    scaled = tuple((running_sum / seq_count for running_sum in totals))
    return (
        block_out,
        layer_input_grad,
        scaled[0],
        scaled[1],
        scaled[2],
        scaled[3],
        scaled[4],
        scaled[5],
        scaled[6],
        scaled[7],
        scaled[8],
        scaled[9],
        scaled[10],
        scaled[11],
        scaled[12],
    )


def solution(mesh):
    placed = (
        P(("rep", "shard"), None),
        P(("rep", "shard"), None),
        P("shard"),
        P("shard"),
        P("shard", None),
        P("shard"),
        P("shard"),
        P("shard", None),
        P("shard"),
        P("shard"),
        P("shard"),
        P("shard", None),
        P("shard"),
        P("shard", None),
        P("shard"),
    )
    return jax.shard_map(
        on_device,
        mesh=mesh,
        in_specs=placed,
        out_specs=(
            P(("rep", "shard"), None),
            P(("rep", "shard"), None),
            P("shard"),
            P("shard"),
            P("shard", None),
            P("shard"),
            P("shard"),
            P("shard", None),
            P("shard"),
            P("shard"),
            P("shard"),
            P("shard", None),
            P("shard"),
            P("shard", None),
            P("shard"),
        ),
        check_vma=False,
    )
```

profile of v0, /device:TPU:0, one launch (start us, length us, event | category | flops | bytes accessed | tf_op | source)
XLA Modules:
  0.0 938.8 jit_solution(5357173971209544075)
XLA Ops:
  10.1 24.7 %all-gather.4 = bf16[8,1,128]{2,1,0:T(2,128)(2,1)S(1)} all-gather(bf16[1,1,128]{2,1,0:T(2,128)(2,1)S(1)} %bitcast.100), channel_id=1, replica_groups=mesh['rep'=16,'shard'=8] {'shard'}, dimensions={0}, use_global_device_ids=true | all-gather | bytes 2304 | tf_op jit(solution)/shard_map/all_gather | solution.py:267
  34.9 18.0 %all-gather.1 = bf16[8,1,128]{2,1,0:T(2,128)(2,1)S(1)} all-gather(bf16[1,1,128]{2,1,0:T(2,128)(2,1)S(1)} %bitcast.101), channel_id=1, replica_groups=mesh['rep'=16,'shard'=8] {'shard'}, dimensions={0}, use_global_device_ids=true | all-gather | bytes 2304 | tf_op jit(solution)/shard_map/all_gather | solution.py:262
  52.9 20.0 %all-gather = bf16[8,1,128]{2,1,0:T(2,128)(2,1)S(1)} all-gather(bf16[1,1,128]{2,1,0:T(2,128)(2,1)S(1)} %bitcast.102), channel_id=1, replica_groups=mesh['rep'=16,'shard'=8] {'shard'}, dimensions={0}, use_global_device_ids=true | all-gather | bytes 2304 | tf_op jit(solution)/shard_map/all_gather | solution.py:261
  72.9 18.0 %all-gather.3 = bf16[8,1,128]{2,1,0:T(2,128)(2,1)S(1)} all-gather(bf16[1,1,128]{2,1,0:T(2,128)(2,1)S(1)} %bitcast.103), channel_id=1, replica_groups=mesh['rep'=16,'shard'=8] {'shard'}, dimensions={0}, use_global_device_ids=true | all-gather | bytes 2304 | tf_op jit(solution)/shard_map/all_gather | solution.py:264
  90.9 20.0 %all-gather.2 = bf16[8,1,128]{2,1,0:T(2,128)(2,1)S(1)} all-gather(bf16[1,1,128]{2,1,0:T(2,128)(2,1)S(1)} %bitcast.104), channel_id=1, replica_groups=mesh['rep'=16,'shard'=8] {'shard'}, dimensions={0}, use_global_device_ids=true | all-gather | bytes 2304 | tf_op jit(solution)/shard_map/all_gather | solution.py:265
  111.0 29.8 %all-gather.7 = bf16[8,1,512]{2,1,0:T(2,128)(2,1)S(1)} all-gather(bf16[1,1,512]{2,1,0:T(2,128)(2,1)S(1)} %reshape.239), channel_id=1, replica_groups=mesh['rep'=16,'shard'=8] {'shard'}, dimensions={0}, use_global_device_ids=true | all-gather | bytes 9216 | tf_op jit(solution)/shard_map/all_gather | solution.py:271
  140.7 18.0 %all-gather.6 = bf16[8,1,128]{2,1,0:T(2,128)(2,1)S(1)} all-gather(bf16[1,1,128]{2,1,0:T(2,128)(2,1)S(1)} %bitcast.105), channel_id=1, replica_groups=mesh['rep'=16,'shard'=8] {'shard'}, dimensions={0}, use_global_device_ids=true | all-gather | bytes 2304 | tf_op jit(solution)/shard_map/all_gather | solution.py:269
  158.8 20.0 %all-gather.5 = bf16[8,1,128]{2,1,0:T(2,128)(2,1)S(1)} all-gather(bf16[1,1,128]{2,1,0:T(2,128)(2,1)S(1)} %bitcast.106), channel_id=1, replica_groups=mesh['rep'=16,'shard'=8] {'shard'}, dimensions={0}, use_global_device_ids=true | all-gather | bytes 2304 | tf_op jit(solution)/shard_map/all_gather | solution.py:268
  180.7 5.1 fusion.39
  185.8 0.9 slice.23
  187.9 1.7 copy.52
  189.6 3.5 fusion.43
  193.1 1.1 exponential_reduce_fusion
  194.3 1.9 copy-done
  196.2 1.3 convolution_convert_fusion.4
  197.5 2.8 fusion.44
  200.7 63.2 %all-gather.18.cloned.1.call-done = bf16[1024,4096]{1,0:T(8,128)(2,1)} async-done(((bf16[128,4096]{1,0:T(8,128)(2,1)}), bf16[1024,4096]{1,0:T(8,128)(2,1)}) %all-gather.18.cloned.1.call-update) | async-done | bytes 8388624 | tf_op jit(solution)/shard_map/all_gather | solution.py:270
  263.9 8.7 convolution_add_fusion
  272.6 98.5 %all-gather.20.cloned.1.call-done = bf16[4096,1024]{1,0:T(8,128)(2,1)} async-done(((bf16[512,1024]{1,0:T(8,128)(2,1)}), bf16[4096,1024]{1,0:T(8,128)(2,1)}) %all-gather.20.cloned.1.call-update) | async-done | bytes 8388624 | tf_op jit(solution)/shard_map/all_gather | solution.py:272
  371.1 9.6 %fusion.45 = (bf16[4096]{0:T(1024)(128)(2,1)}, bf16[320,4096]{1,0:T(8,128)(2,1)S(1)}) fusion(f32[320,4096]{1,0:T(8,128)} %convolution_add_fusion, bf16[4096,1024]{1,0:T(8,128)(2,1)} %all-gather.20.cloned.1.call-done, f32[320,1024]{1,0:T(8,128)S(1)} %copy-done.17), kind=kOutput, calls=%fused_computation.102 | convolution fusion | flops 2710892544 | bytes 17571840 | tf_op jit(solution)/shard_map/dot_general | solution.py:175
  380.7 3.8 multiply_reduce_fusion.1
  384.5 1.1 fusion.41
  385.6 2.6 convolution_convert_fusion.3
  388.4 2.5 convolution_convert_fusion.5
  390.9 1.2 copy.54
  392.1 8.6 multiply_reduce_fusion
  400.7 6.9 multiply_convert_fusion
  407.7 3.9 multiply_convert_fusion.2
  413.1 2.5 bitcast_convert_fusion
  416.5 8.3 convolution_convert_fusion.2
  425.0 1.0 copy-done.3
  426.0 8.7 convolution_convert_fusion.1
  434.8 1.2 copy-done.19
  436.0 10.3 %convolution_convert_fusion = bf16[4096,1024]{1,0:T(8,128)(2,1)} fusion(f32[320,1024]{1,0:T(8,128)S(1)} %copy-done.19, f32[320,4096]{1,0:T(8,128)} %convolution_add_fusion), kind=kOutput, calls=%fused_computation.7 | convolution fusion | flops 2700673024 | bytes 14942208 | tf_op jit(solution)/shard_map/dot_general | solution.py:174
  446.4 18.7 %all-gather.8 = bf16[8,1,128]{2,1,0:T(2,128)(2,1)S(1)} all-gather(bf16[1,1,128]{2,1,0:T(2,128)(2,1)} %bitcast.107), channel_id=1, replica_groups=mesh['rep'=16,'shard'=8] {'shard'}, dimensions={0}, use_global_device_ids=true | all-gather | bytes 2304 | tf_op jit(solution)/shard_map/all_gather | solution.py:273
  465.8 1.2 dynamic-slice
  469.3 7.4 fusion.21
  476.7 38.7 %all-reduce.11 = (bf16[1024]{0:T(1024)(128)(2,1)S(1)}, bf16[1024]{0:T(1024)(128)(2,1)S(1)}, bf16[1024]{0:T(1024)(128)(2,1)S(1)}, bf16[1024]{0:T(1024)(128)(2,1)S...) all-reduce(bf16[1024]{0:T(1024)(128)(2,1)S(1)} %get-tuple-element.1, ...), channel_id=2, replica_groups=mesh['rep'=16,'shard'=8] {'shard'}, use_global_device_ids=true, to_apply=%region_12.13.clone | all-reduce | flops 12288 | bytes 49152
  516.1 28.3 %all-reduce.9 = (bf16[128]{0:T(256)(128)(2,1)S(1)}, bf16[128]{0:T(256)(128)(2,1)S(1)}, bf16[128]{0:T(256)(128)(2,1)S(1)}, bf16[128]{0:T(256)(128)(2,1)S(1)}, bf1...) all-reduce(bf16[128]{0:T(256)(128)(2,1)S(1)} %dynamic-slice.1, ...), channel_id=1, replica_groups=mesh['rep'=16,'shard'=8] {'rep'}, use_global_device_ids=true, to_apply=%region_13.14 | all-reduce | flops 1536 | bytes 6144 | tf_op jit(solution)/shard_map/psum | solution.py:334
  547.0 16.4 %reduce-scatter.5.cloned.1.call-done = bf16[128,3072]{1,0:T(8,128)(2,1)} async-done(((bf16[1024,3072]{1,0:T(8,128)(2,1)}), bf16[128,3072]{1,0:T(8,128)(2,1)}) %reduce-scatter.5.cloned.1.call-update) | async-done | bytes 786448 | tf_op jit(solution)/shard_map/reduce_scatter | solution.py:299
  563.4 117.0 %reduce-scatter.9.cloned.1.call-done = bf16[128,4096]{1,0:T(8,128)(2,1)} async-done(((bf16[1024,4096]{1,0:T(8,128)(2,1)}), bf16[128,4096]{1,0:T(8,128)(2,1)}) %reduce-scatter.9.cloned.1.call-update) | async-done | bytes 1048592 | tf_op jit(solution)/shard_map/reduce_scatter | solution.py:320
  680.3 116.9 %reduce-scatter.11.cloned.1.call-done = bf16[512,1024]{1,0:T(8,128)(2,1)} async-done(((bf16[4096,1024]{1,0:T(8,128)(2,1)}), bf16[512,1024]{1,0:T(8,128)(2,1)}) %reduce-scatter.11.cloned.1.call-update) | async-done | bytes 1048592 | tf_op jit(solution)/shard_map/reduce_scatter | solution.py:326
  799.4 2.8 fusion.20
  802.2 9.3 fusion.14
  811.5 113.9 %all-reduce.14.cloned.1.call-done = (bf16[128,3072]{1,0:T(8,128)(2,1)}, bf16[128,1024]{1,0:T(8,128)(2,1)}, bf16[128,4096]{1,0:T(8,128)(2,1)}, bf16[512,1024]{1,0:T(8,128)(2,1)}) async-done(((bf16[128,3072]{1,0:T(8,128)(2,1)}, bf16[128,1024]{1,0:T(8,128)(2,1)}, bf16[128,4096]{1,0:T(8,128)(2,1)}, bf16[512,1024]{1,0:T(8,128)(2,1)}), (bf16[128,3072]{1,0:T(8,128)(2,1)}, bf16[128,1024]{1,0:T(8,128)(2,1)}, ...) | async-done | bytes 3145744 | tf_op jit(solution)/shard_map/psum | solution.py:336
  925.4 2.5 convert_multiply_fusion.2
  928.8 1.5 convert_multiply_fusion.1
  930.4 1.6 convert_multiply_fusion
  (173 shorter events, 17.0 us)
Async XLA Ops:
  7.2 27.7 %copy-start.41 = (bf16[128]{0:T(256)(128)(2,1)S(1)}, bf16[128]{0:T(256)(128)(2,1)}, u32[]{:S(2)}) copy-start(bf16[128]{0:T(256)(128)(2,1)} %param.18) | copy-start | bytes 772
  7.2 45.7 %copy-start.42 = (bf16[128]{0:T(256)(128)(2,1)S(1)}, bf16[128]{0:T(256)(128)(2,1)}, u32[]{:S(2)}) copy-start(bf16[128]{0:T(256)(128)(2,1)} %param.17) | copy-start | bytes 772
  7.2 65.7 %copy-start.43 = (bf16[128]{0:T(256)(128)(2,1)S(1)}, bf16[128]{0:T(256)(128)(2,1)}, u32[]{:S(2)}) copy-start(bf16[128]{0:T(256)(128)(2,1)} %param.20) | copy-start | bytes 772
  7.2 83.7 %copy-start.44 = (bf16[128]{0:T(256)(128)(2,1)S(1)}, bf16[128]{0:T(256)(128)(2,1)}, u32[]{:S(2)}) copy-start(bf16[128]{0:T(256)(128)(2,1)} %param.21) | copy-start | bytes 772
  7.2 103.7 %copy-start.39 = (bf16[512]{0:T(512)(128)(2,1)S(1)}, bf16[512]{0:T(512)(128)(2,1)}, u32[]{:S(2)}) copy-start(bf16[512]{0:T(512)(128)(2,1)} %param.27) | copy-start | bytes 3076
  7.2 133.5 %copy-start.45 = (bf16[128]{0:T(256)(128)(2,1)S(1)}, bf16[128]{0:T(256)(128)(2,1)}, u32[]{:S(2)}) copy-start(bf16[128]{0:T(256)(128)(2,1)} %param.25) | copy-start | bytes 772
  7.3 151.5 %copy-start.46 = (bf16[128]{0:T(256)(128)(2,1)S(1)}, bf16[128]{0:T(256)(128)(2,1)}, u32[]{:S(2)}) copy-start(bf16[128]{0:T(256)(128)(2,1)} %param.24) | copy-start | bytes 772
  7.3 172.8 %copy-start.6 = (bf16[320,1024]{1,0:T(8,128)(2,1)S(1)}, bf16[320,1024]{1,0:T(8,128)(2,1)}, u32[]{:S(2)}) copy-start(bf16[320,1024]{1,0:T(8,128)(2,1)} %param.15) | copy-start | bytes 1966084
  7.3 173.4 %all-gather.14.cloned.1.call-start = ((), (), s32[]{:S(2)}) async-start(), calls=%async_computation.4 | async-start | bytes 7077888 | tf_op jit(solution)/shard_map/all_gather | solution.py:263
  8.0 189.5 %all-gather.16.cloned.1.call-start = ((), (), s32[]{:S(2)}) async-start(), calls=%async_computation.5 | async-start | bytes 2359296 | tf_op jit(solution)/shard_map/all_gather | solution.py:266
  8.8 255.1 %all-gather.18.cloned.1.call-start = ((), (), s32[]{:S(2)}) async-start(), calls=%async_computation.6 | async-start | bytes 9437184 | tf_op jit(solution)/shard_map/all_gather | solution.py:270
  9.5 361.6 %all-gather.20.cloned.1.call-start = ((), (), s32[]{:S(2)}) async-start(), calls=%async_computation.7 | async-start | bytes 9437184 | tf_op jit(solution)/shard_map/all_gather | solution.py:272
  10.1 536.9 %reduce-scatter.7.cloned.1.call-start = ((), (), s32[]{:S(2)}) async-start(), calls=%async_computation.9 | async-start | bytes 2359296 | tf_op jit(solution)/shard_map/reduce_scatter | solution.py:308
  52.9 132.9 %copy-start.33 = (f32[8,1,128]{2,1,0:T(1,128)}, f32[8,1,128]{2,1,0:T(1,128)S(1)}, u32[]{:S(2)}) copy-start(f32[8,1,128]{2,1,0:T(1,128)S(1)} %convert_element_type.271) | copy-start | bytes 12292
  158.8 105.1 %copy-start.35 = (f32[8,1,128]{2,1,0:T(1,128)}, f32[8,1,128]{2,1,0:T(1,128)S(1)}, u32[]{:S(2)}) copy-start(f32[8,1,128]{2,1,0:T(1,128)S(1)} %convert_element_type.276) | copy-start | bytes 12292
  180.6 5.2 copy-start.27
  187.5 6.8 copy-start.10
  187.9 5.3 copy-start.16
  189.6 3.5 copy-start.14
  193.1 3.0 copy-start
  200.3 184.1 %copy-start.2 = (f32[320,1024]{1,0:T(8,128)}, f32[320,1024]{1,0:T(8,128)S(1)}, u32[]{:S(2)}) copy-start(f32[320,1024]{1,0:T(8,128)S(1)} %get-tuple-element.55) | copy-start | bytes 3932164
  263.9 107.2 %copy-start.17 = (f32[320,1024]{1,0:T(8,128)S(1)}, f32[320,1024]{1,0:T(8,128)}, u32[]{:S(2)}) copy-start(f32[320,1024]{1,0:T(8,128)} %param.16) | copy-start | bytes 3932164
  371.1 9.6 %copy-start.47 = (bf16[1024,4096]{1,0:T(8,128)(2,1)S(1)}, bf16[1024,4096]{1,0:T(8,128)(2,1)}, u32[]{:S(2)}) copy-start(bf16[1024,4096]{1,0:T(8,128)(2,1)} %all-gather.18.cloned.1.call-done) | copy-start | bytes 25165828
  380.7 3.8 copy-start.49
  380.7 3.8 copy-start.18
  388.2 175.2 %reduce-scatter.5.cloned.1.call-start = ((), (), s32[]{:S(2)}) async-start(), calls=%async_computation.8 | async-start | bytes 7077888 | tf_op jit(solution)/shard_map/reduce_scatter | solution.py:299
  392.1 8.6 slice-start
  392.1 8.6 slice-start.1
  407.6 4.0 copy-start.1
  407.7 4.0 copy-start.15
  411.6 3.9 copy-start.24
  413.1 3.4 copy-start.7
  413.1 3.4 copy-start.28
  413.1 3.4 copy-start.34
  424.8 255.6 %reduce-scatter.9.cloned.1.call-start = ((), (), s32[]{:S(2)}) async-start(), calls=%async_computation.10 | async-start | bytes 9437184 | tf_op jit(solution)/shard_map/reduce_scatter | solution.py:320
  434.8 362.4 %reduce-scatter.11.cloned.1.call-start = ((), (), s32[]{:S(2)}) async-start(), calls=%async_computation.11 | async-start | bytes 9437184 | tf_op jit(solution)/shard_map/reduce_scatter | solution.py:326
  446.3 22.6 %copy-start.13 = (f32[16,64,320]{2,1,0:T(8,128)S(1)}, f32[16,64,320]{2,1,0:T(8,128)}, u32[]{:S(2)}) copy-start(f32[16,64,320]{2,1,0:T(8,128)} %get-tuple-element.58) | copy-start | bytes 3932164
  446.3 22.9 %copy-start.8 = (bf16[320,1024]{1,0:T(8,128)(2,1)S(1)}, bf16[320,1024]{1,0:T(8,128)(2,1)}, u32[]{:S(2)}) copy-start(bf16[320,1024]{1,0:T(8,128)(2,1)} %param.15) | copy-start | bytes 1966084
  446.4 479.1 %all-reduce.14.cloned.1.call-start = ((), (), s32[]{:S(2)}) async-start(), calls=%async_computation.12 | async-start | bytes 6291456 | tf_op jit(solution)/shard_map/psum | solution.py:336
  469.3 7.4 copy-start.26
  469.3 7.4 copy-start.30
  469.3 7.4 copy-start.31
  469.3 7.4 copy-start.37
  469.3 7.4 copy-start.38
  476.7 322.7 %copy-start.5 = (f32[320,1024]{1,0:T(8,128)S(1)}, f32[320,1024]{1,0:T(8,128)}, u32[]{:S(2)}) copy-start(f32[320,1024]{1,0:T(8,128)} %copy-done.4) | copy-start | bytes 3932164
  476.7 322.7 %copy-start.29 = (f32[320]{0:T(512)S(1)}, f32[320]{0:T(512)}, u32[]{:S(2)}) copy-start(f32[320]{0:T(512)} %copy-done.27) | copy-start | bytes 3844
  797.2 5.0 copy-start.32
  925.4 3.4 copy-start.21
  (13 other events, 26.0 us)
Sparse Core Ops, SparseCore 0:
  10.4 91.6 all-gather.13
  104.5 51.9 all-gather.15
  158.8 104.9 all-gather.17
  266.1 104.9 all-gather.19
  388.3 72.8 reduce-scatter.6
  464.9 98.3 reduce-scatter.4
  567.2 113.1 reduce-scatter.8
  684.6 112.5 reduce-scatter.10
  800.0 125.3 all-reduce.13
where the time goes:
time: 947 us; the launch traced here: 939 us
  waiting for transfers between devices  529 us (56%)
  blocking collectives  254 us (27%)
  matrix products  99.6 us (11%)
  other arithmetic  26.6 us (3%)
  between operations  16 us (2%)
  local copies, waits for them, and re-layouts  12.9 us (1%)
    reduce_scatter x1, waiting for transfers between devices, on_device(): lax.psum_scatter(grads[9].astype(jnp.bfloat16), 'shard', scatter_dimensio...  117 us
    reduce_scatter x1, waiting for transfers between devices, on_device(): lax.psum_scatter(grads[11].astype(jnp.bfloat16), 'shard', scatter_dimensi...  117 us
    psum x1, waiting for transfers between devices, on_device(): lax.psum(shares[2].astype(jnp.bfloat16), 'rep').astype(jnp.float32)  114 us
    all_gather x1, waiting for transfers between devices, on_device(): lax.all_gather(w_down, 'shard', axis=0, tiled=True)  98.5 us
    all_gather x1, waiting for transfers between devices, on_device(): lax.all_gather(w_up, 'shard', axis=0, tiled=True)  63.2 us
    unnamed x1, blocking collectives  38.7 us
    all_gather x1, blocking collectives, on_device(): lax.all_gather(up_bias, 'shard', axis=0, tiled=True)  29.8 us
    psum x1, blocking collectives, on_device(): lax.psum(shares[0].astype(jnp.bfloat16), 'rep').astype(jnp.float32)  28.3 us
  transfers between devices with their start and end apart: 9, of which 6 were waited for; matrix products, arithmetic and copies ran while one was open for 12% of the time, Pallas kernels for 0%

commit v1 on v0

--- a/solution.py
+++ b/solution.py
@@ -333,7 +333,7 @@
     totals = (
         lax.psum(shares[0].astype(jnp.bfloat16), "rep").astype(jnp.float32),
         lax.psum(shares[1].astype(jnp.bfloat16), "rep").astype(jnp.float32),
-        lax.psum(shares[2].astype(jnp.bfloat16), "rep").astype(jnp.float32),
+        jnp.sum(lax.all_gather(shares[2].astype(jnp.bfloat16), "rep"), axis=0).astype(jnp.float32),
         lax.psum(shares[3].astype(jnp.bfloat16), "rep").astype(jnp.float32),
         lax.psum(shares[4].astype(jnp.bfloat16), "rep").astype(jnp.float32),
         lax.psum(shares[5].astype(jnp.bfloat16), "rep").astype(jnp.float32),

time: 947 us -> 1020 us (1.077)
  waiting for transfers between devices: 529 us -> 595 us
    psum x1, waiting for transfers between devices: 114 us -> 13.4 us  [on_device(): lax.psum(shares[5].astype(jnp.bfloat16), 'rep').astype(jnp.float32)]
    reduce_scatter x1, waiting for transfers between devices: 16.4 us -> 100 us  [on_device(): lax.psum_scatter(grads[2].astype(jnp.bfloat16), 'shard', scatter_dimensio...]
    all_gather x0 -> x1, waiting for transfers between devices: none -> 67.6 us  [on_device(): lax.all_gather(shares[2].astype(jnp.bfloat16), 'rep')]
    reduce_scatter x1, waiting for transfers between devices: 0.01 us -> 15.7 us  [on_device(): lax.psum_scatter(grads[5].astype(jnp.bfloat16), 'shard', scatter_dimensio...]
  transfers between devices with their start and end apart: 9 -> 10, of which waited for: 6 -> 8; matrix products, arithmetic and copies ran while one was open for 12% -> 11% of each run, Pallas kernels for 0% -> 0%
where the time goes in v1:
time: 1020 us; the launch traced here: 1010 us
  waiting for transfers between devices  595 us (58%)
  blocking collectives  254 us (25%)
  matrix products  98.7 us (10%)
  other arithmetic  34.7 us (3%)
  between operations  16.5 us (2%)
  local copies, waits for them, and re-layouts  10.6 us (1%)
    reduce_scatter x1, waiting for transfers between devices, on_device(): lax.psum_scatter(grads[11].astype(jnp.bfloat16), 'shard', scatter_dimensi...  117 us
    reduce_scatter x1, waiting for transfers between devices, on_device(): lax.psum_scatter(grads[9].astype(jnp.bfloat16), 'shard', scatter_dimensio...  117 us
    reduce_scatter x1, waiting for transfers between devices, on_device(): lax.psum_scatter(grads[2].astype(jnp.bfloat16), 'shard', scatter_dimensio...  100 us
    all_gather x1, waiting for transfers between devices, on_device(): lax.all_gather(w_down, 'shard', axis=0, tiled=True)  98.8 us
    all_gather x1, waiting for transfers between devices, on_device(): lax.all_gather(shares[2].astype(jnp.bfloat16), 'rep')  67.6 us
    all_gather x1, waiting for transfers between devices, on_device(): lax.all_gather(w_up, 'shard', axis=0, tiled=True)  62.8 us
    unnamed x1, blocking collectives  37.1 us
    all_gather x1, blocking collectives, on_device(): lax.all_gather(up_bias, 'shard', axis=0, tiled=True)  29.8 us
  transfers between devices with their start and end apart: 10, of which 8 were waited for; matrix products, arithmetic and copies ran while one was open for 11% of the time, Pallas kernels for 0%

profile of v1, /device:TPU:0, one launch (start us, length us, event | category | flops | bytes accessed | tf_op | source)
XLA Modules:
  0.0 1009.5 jit_solution(644155333772538516)
XLA Ops:
  10.1 24.7 %all-gather.5 = bf16[8,1,128]{2,1,0:T(2,128)(2,1)S(1)} all-gather(bf16[1,1,128]{2,1,0:T(2,128)(2,1)S(1)} %bitcast.102), channel_id=1, replica_groups=mesh['rep'=16,'shard'=8] {'shard'}, dimensions={0}, use_global_device_ids=true | all-gather | bytes 2304 | tf_op jit(solution)/shard_map/all_gather | solution.py:267
  34.9 18.0 %all-gather.2 = bf16[8,1,128]{2,1,0:T(2,128)(2,1)S(1)} all-gather(bf16[1,1,128]{2,1,0:T(2,128)(2,1)S(1)} %bitcast.103), channel_id=1, replica_groups=mesh['rep'=16,'shard'=8] {'shard'}, dimensions={0}, use_global_device_ids=true | all-gather | bytes 2304 | tf_op jit(solution)/shard_map/all_gather | solution.py:262
  52.9 20.0 %all-gather.1 = bf16[8,1,128]{2,1,0:T(2,128)(2,1)S(1)} all-gather(bf16[1,1,128]{2,1,0:T(2,128)(2,1)S(1)} %bitcast.104), channel_id=1, replica_groups=mesh['rep'=16,'shard'=8] {'shard'}, dimensions={0}, use_global_device_ids=true | all-gather | bytes 2304 | tf_op jit(solution)/shard_map/all_gather | solution.py:261
  72.9 18.0 %all-gather.4 = bf16[8,1,128]{2,1,0:T(2,128)(2,1)S(1)} all-gather(bf16[1,1,128]{2,1,0:T(2,128)(2,1)S(1)} %bitcast.105), channel_id=1, replica_groups=mesh['rep'=16,'shard'=8] {'shard'}, dimensions={0}, use_global_device_ids=true | all-gather | bytes 2304 | tf_op jit(solution)/shard_map/all_gather | solution.py:264
  90.9 20.0 %all-gather.3 = bf16[8,1,128]{2,1,0:T(2,128)(2,1)S(1)} all-gather(bf16[1,1,128]{2,1,0:T(2,128)(2,1)S(1)} %bitcast.106), channel_id=1, replica_groups=mesh['rep'=16,'shard'=8] {'shard'}, dimensions={0}, use_global_device_ids=true | all-gather | bytes 2304 | tf_op jit(solution)/shard_map/all_gather | solution.py:265
  110.9 29.8 %all-gather.8 = bf16[8,1,512]{2,1,0:T(2,128)(2,1)S(1)} all-gather(bf16[1,1,512]{2,1,0:T(2,128)(2,1)S(1)} %reshape.240), channel_id=1, replica_groups=mesh['rep'=16,'shard'=8] {'shard'}, dimensions={0}, use_global_device_ids=true | all-gather | bytes 9216 | tf_op jit(solution)/shard_map/all_gather | solution.py:271
  141.3 18.0 %all-gather.7 = bf16[8,1,128]{2,1,0:T(2,128)(2,1)S(1)} all-gather(bf16[1,1,128]{2,1,0:T(2,128)(2,1)S(1)} %bitcast.107), channel_id=1, replica_groups=mesh['rep'=16,'shard'=8] {'shard'}, dimensions={0}, use_global_device_ids=true | all-gather | bytes 2304 | tf_op jit(solution)/shard_map/all_gather | solution.py:269
  159.9 20.0 %all-gather.6 = bf16[8,1,128]{2,1,0:T(2,128)(2,1)S(1)} all-gather(bf16[1,1,128]{2,1,0:T(2,128)(2,1)S(1)} %bitcast.108), channel_id=1, replica_groups=mesh['rep'=16,'shard'=8] {'shard'}, dimensions={0}, use_global_device_ids=true | all-gather | bytes 2304 | tf_op jit(solution)/shard_map/all_gather | solution.py:268
  181.3 5.1 fusion.39
  188.5 1.7 copy.52
  190.3 3.5 fusion.43
  193.8 1.2 exponential_reduce_fusion
  195.0 1.9 copy-done
  196.9 1.3 convolution_convert_fusion.4
  198.2 2.6 fusion.44
  201.1 62.8 %all-gather.20.cloned.1.call-done = bf16[1024,4096]{1,0:T(8,128)(2,1)} async-done(((bf16[128,4096]{1,0:T(8,128)(2,1)}), bf16[1024,4096]{1,0:T(8,128)(2,1)}) %all-gather.20.cloned.1.call-update) | async-done | bytes 8388624 | tf_op jit(solution)/shard_map/all_gather | solution.py:270
  263.9 8.5 convolution_add_fusion
  272.4 98.8 %all-gather.22.cloned.1.call-done = bf16[4096,1024]{1,0:T(8,128)(2,1)} async-done(((bf16[512,1024]{1,0:T(8,128)(2,1)}), bf16[4096,1024]{1,0:T(8,128)(2,1)}) %all-gather.22.cloned.1.call-update) | async-done | bytes 8388624 | tf_op jit(solution)/shard_map/all_gather | solution.py:272
  371.1 9.0 fusion.45
  380.1 3.3 multiply_reduce_fusion.1
  384.0 2.6 convolution_convert_fusion.3
  386.7 8.9 convolution_convert_fusion.1
  395.6 1.2 copy-done.17
  396.9 10.4 %convolution_convert_fusion = bf16[4096,1024]{1,0:T(8,128)(2,1)} fusion(f32[320,1024]{1,0:T(8,128)S(1)} %copy-done.17, f32[320,4096]{1,0:T(8,128)} %convolution_add_fusion), kind=kOutput, calls=%fused_computation.7 | convolution fusion | flops 2700673024 | bytes 14942208 | tf_op jit(solution)/shard_map/dot_general | solution.py:174
  407.4 2.5 convolution_convert_fusion.5
  409.9 1.2 copy.54
  411.1 8.5 multiply_reduce_fusion
  419.6 7.0 multiply_convert_fusion
  426.6 3.9 multiply_convert_fusion.2
  432.0 2.5 bitcast_convert_fusion
  435.4 8.5 convolution_convert_fusion.2
  444.0 15.7 %reduce-scatter.7.cloned.1.call-done = bf16[128,1024]{1,0:T(8,128)(2,1)} async-done(((bf16[1024,1024]{1,0:T(8,128)(2,1)}), bf16[128,1024]{1,0:T(8,128)(2,1)}) %reduce-scatter.7.cloned.1.call-update) | async-done | bytes 262160 | tf_op jit(solution)/shard_map/reduce_scatter | solution.py:308
  459.6 116.5 %reduce-scatter.9.cloned.1.call-done = bf16[128,4096]{1,0:T(8,128)(2,1)} async-done(((bf16[1024,4096]{1,0:T(8,128)(2,1)}), bf16[128,4096]{1,0:T(8,128)(2,1)}) %reduce-scatter.9.cloned.1.call-update) | async-done | bytes 1048592 | tf_op jit(solution)/shard_map/reduce_scatter | solution.py:320
  576.2 117.3 %reduce-scatter.11.cloned.1.call-done = bf16[512,1024]{1,0:T(8,128)(2,1)} async-done(((bf16[4096,1024]{1,0:T(8,128)(2,1)}), bf16[512,1024]{1,0:T(8,128)(2,1)}) %reduce-scatter.11.cloned.1.call-update) | async-done | bytes 1048592 | tf_op jit(solution)/shard_map/reduce_scatter | solution.py:326
  693.5 100.3 %reduce-scatter.5.cloned.1.call-done = bf16[128,3072]{1,0:T(8,128)(2,1)} async-done(((bf16[1024,3072]{1,0:T(8,128)(2,1)}), bf16[128,3072]{1,0:T(8,128)(2,1)}) %reduce-scatter.5.cloned.1.call-update) | async-done | bytes 786448 | tf_op jit(solution)/shard_map/reduce_scatter | solution.py:299
  793.8 19.9 %all-gather.9 = bf16[8,1,128]{2,1,0:T(2,128)(2,1)S(1)} all-gather(bf16[1,1,128]{2,1,0:T(2,128)(2,1)S(1)} %bitcast.109), channel_id=1, replica_groups=mesh['rep'=16,'shard'=8] {'shard'}, dimensions={0}, use_global_device_ids=true | all-gather | bytes 2304 | tf_op jit(solution)/shard_map/all_gather | solution.py:273
  816.1 7.6 fusion.21
  823.7 37.1 %all-reduce.11 = (bf16[1024]{0:T(1024)(128)(2,1)S(1)}, bf16[1024]{0:T(1024)(128)(2,1)S(1)}, bf16[1024]{0:T(1024)(128)(2,1)S(1)}, bf16[1024]{0:T(1024)(128)(2,1)S...) all-reduce(bf16[1024]{0:T(1024)(128)(2,1)S(1)} %get-tuple-element.1, ...), channel_id=3, replica_groups=mesh['rep'=16,'shard'=8] {'shard'}, use_global_device_ids=true, to_apply=%region_12.13.clone | all-reduce | flops 12288 | bytes 49152
  861.4 28.1 %all-reduce.9 = (bf16[128]{0:T(256)(128)(2,1)S(1)}, bf16[128]{0:T(256)(128)(2,1)S(1)}, bf16[128]{0:T(256)(128)(2,1)S(1)}, bf16[128]{0:T(256)(128)(2,1)S(1)}, bf1...) all-reduce(bf16[128]{0:T(256)(128)(2,1)S(1)} %dynamic-slice.1, ...), channel_id=1, replica_groups=mesh['rep'=16,'shard'=8] {'rep'}, use_global_device_ids=true, to_apply=%region_13.14 | all-reduce | flops 1536 | bytes 6144 | tf_op jit(solution)/shard_map/psum | solution.py:334
  894.2 2.8 fusion.20
  897.1 9.2 fusion.14
  906.3 13.4 %all-reduce.14.cloned.1.call-done = (bf16[128,1024]{1,0:T(8,128)(2,1)}, bf16[128,4096]{1,0:T(8,128)(2,1)}, bf16[512,1024]{1,0:T(8,128)(2,1)}) async-done(((bf16[128,1024]{1,0:T(8,128)(2,1)}, bf16[128,4096]{1,0:T(8,128)(2,1)}, bf16[512,1024]{1,0:T(8,128)(2,1)}), (bf16[128,1024]{1,0:T(8,128)(2,1)}, bf16[128,4096]{1,0:T(8,128)(2,1)}, bf16[512,1024]{1,0:T(8,128)(2,1)})) %all-reduce.14.cloned.1.call-update) | async-done | bytes 2359312 | tf_op jit(solution)/shard_map/psum | solution.py:339
  919.7 1.9 convert_multiply_fusion.3
  921.6 2.8 convert_multiply_fusion
  924.4 1.5 convert_multiply_fusion.1
  925.9 67.6 %all-gather.24.cloned.1.call-done = bf16[2048,3072]{1,0:T(8,128)(2,1)} async-done(((bf16[128,3072]{1,0:T(8,128)(2,1)}), bf16[2048,3072]{1,0:T(8,128)(2,1)}) %all-gather.24.cloned.1.call-update) | async-done | bytes 12582928 | tf_op jit(solution)/shard_map/all_gather | solution.py:336
  993.5 7.4 reduce_sum.195
  1000.9 1.3 convert_multiply_fusion.2
  (157 shorter events, 17.4 us)
Async XLA Ops:
  7.2 2.9 copy-start.29
  7.2 27.7 %copy-start.30 = (bf16[128]{0:T(256)(128)(2,1)S(1)}, bf16[128]{0:T(256)(128)(2,1)}, u32[]{:S(2)}) copy-start(bf16[128]{0:T(256)(128)(2,1)} %param.18) | copy-start | bytes 772
  7.2 45.7 %copy-start.31 = (bf16[128]{0:T(256)(128)(2,1)S(1)}, bf16[128]{0:T(256)(128)(2,1)}, u32[]{:S(2)}) copy-start(bf16[128]{0:T(256)(128)(2,1)} %param.17) | copy-start | bytes 772
  7.2 65.7 %copy-start.32 = (bf16[128]{0:T(256)(128)(2,1)S(1)}, bf16[128]{0:T(256)(128)(2,1)}, u32[]{:S(2)}) copy-start(bf16[128]{0:T(256)(128)(2,1)} %param.20) | copy-start | bytes 772
  7.2 83.7 %copy-start.33 = (bf16[128]{0:T(256)(128)(2,1)S(1)}, bf16[128]{0:T(256)(128)(2,1)}, u32[]{:S(2)}) copy-start(bf16[128]{0:T(256)(128)(2,1)} %param.21) | copy-start | bytes 772
  7.2 103.7 %copy-start.28 = (bf16[512]{0:T(512)(128)(2,1)S(1)}, bf16[512]{0:T(512)(128)(2,1)}, u32[]{:S(2)}) copy-start(bf16[512]{0:T(512)(128)(2,1)} %param.27) | copy-start | bytes 3076
  7.2 134.1 %copy-start.34 = (bf16[128]{0:T(256)(128)(2,1)S(1)}, bf16[128]{0:T(256)(128)(2,1)}, u32[]{:S(2)}) copy-start(bf16[128]{0:T(256)(128)(2,1)} %param.25) | copy-start | bytes 772
  7.3 152.7 %copy-start.35 = (bf16[128]{0:T(256)(128)(2,1)S(1)}, bf16[128]{0:T(256)(128)(2,1)}, u32[]{:S(2)}) copy-start(bf16[128]{0:T(256)(128)(2,1)} %param.24) | copy-start | bytes 772
  7.3 173.5 %copy-start.6 = (bf16[320,1024]{1,0:T(8,128)(2,1)S(1)}, bf16[320,1024]{1,0:T(8,128)(2,1)}, u32[]{:S(2)}) copy-start(bf16[320,1024]{1,0:T(8,128)(2,1)} %param.15) | copy-start | bytes 1966084
  7.3 174.0 %all-gather.16.cloned.1.call-start = ((), (), s32[]{:S(2)}) async-start(), calls=%async_computation.4 | async-start | bytes 7077888 | tf_op jit(solution)/shard_map/all_gather | solution.py:263
  8.0 190.2 %all-gather.18.cloned.1.call-start = ((), (), s32[]{:S(2)}) async-start(), calls=%async_computation.5 | async-start | bytes 2359296 | tf_op jit(solution)/shard_map/all_gather | solution.py:266
  8.8 255.1 %all-gather.20.cloned.1.call-start = ((), (), s32[]{:S(2)}) async-start(), calls=%async_computation.6 | async-start | bytes 9437184 | tf_op jit(solution)/shard_map/all_gather | solution.py:270
  9.5 361.6 %all-gather.22.cloned.1.call-start = ((), (), s32[]{:S(2)}) async-start(), calls=%async_computation.7 | async-start | bytes 9437184 | tf_op jit(solution)/shard_map/all_gather | solution.py:272
  10.1 449.6 %reduce-scatter.7.cloned.1.call-start = ((), (), s32[]{:S(2)}) async-start(), calls=%async_computation.9 | async-start | bytes 2359296 | tf_op jit(solution)/shard_map/reduce_scatter | solution.py:308
  52.9 133.6 %copy-start.25 = (f32[8,1,128]{2,1,0:T(1,128)}, f32[8,1,128]{2,1,0:T(1,128)S(1)}, u32[]{:S(2)}) copy-start(f32[8,1,128]{2,1,0:T(1,128)S(1)} %convert_element_type.273) | copy-start | bytes 12292
  181.3 5.2 copy-start.23
  188.1 6.8 copy-start.10
  188.5 5.2 copy-start.14
  190.3 3.5 copy-start.12
  193.8 3.1 copy-start
  198.2 65.7 %copy-start.22 = (f32[8,1,512]{2,1,0:T(1,128)S(1)}, f32[8,1,512]{2,1,0:T(1,128)}, u32[]{:S(2)}) copy-start(f32[8,1,512]{2,1,0:T(1,128)} %convert_element_type.279) | copy-start | bytes 49156
  198.2 65.7 %copy-start.27 = (f32[8,1,128]{2,1,0:T(1,128)S(1)}, f32[8,1,128]{2,1,0:T(1,128)}, u32[]{:S(2)}) copy-start(f32[8,1,128]{2,1,0:T(1,128)} %convert_element_type.278) | copy-start | bytes 12292
  200.8 185.9 %copy-start.2 = (f32[320,1024]{1,0:T(8,128)}, f32[320,1024]{1,0:T(8,128)S(1)}, u32[]{:S(2)}) copy-start(f32[320,1024]{1,0:T(8,128)S(1)} %get-tuple-element.54) | copy-start | bytes 3932164
  263.9 107.2 %copy-start.15 = (f32[320,1024]{1,0:T(8,128)S(1)}, f32[320,1024]{1,0:T(8,128)}, u32[]{:S(2)}) copy-start(f32[320,1024]{1,0:T(8,128)} %param.16) | copy-start | bytes 3932164
  371.1 9.0 copy-start.37
  380.1 3.3 copy-start.39
  380.1 3.3 copy-start.16
  384.0 23.4 %copy-start.4 = (f32[320,1024]{1,0:T(8,128)}, f32[320,1024]{1,0:T(8,128)S(1)}, u32[]{:S(2)}) copy-start(f32[320,1024]{1,0:T(8,128)S(1)} %get-tuple-element.45) | copy-start | bytes 3932164
  386.6 189.6 %reduce-scatter.9.cloned.1.call-start = ((), (), s32[]{:S(2)}) async-start(), calls=%async_computation.10 | async-start | bytes 9437184 | tf_op jit(solution)/shard_map/reduce_scatter | solution.py:320
  395.6 297.9 %reduce-scatter.11.cloned.1.call-start = ((), (), s32[]{:S(2)}) async-start(), calls=%async_computation.11 | async-start | bytes 9437184 | tf_op jit(solution)/shard_map/reduce_scatter | solution.py:326
  407.3 386.5 %reduce-scatter.5.cloned.1.call-start = ((), (), s32[]{:S(2)}) async-start(), calls=%async_computation.8 | async-start | bytes 7077888 | tf_op jit(solution)/shard_map/reduce_scatter | solution.py:299
  411.1 8.5 slice-start
  411.1 8.5 slice-start.1
  426.6 3.9 copy-start.1
  426.6 3.9 copy-start.13
  430.5 3.9 copy-start.21
  432.0 3.4 copy-start.7
  432.0 3.4 copy-start.24
  432.0 3.4 copy-start.26
  443.9 349.9 %copy-start.36 = (bf16[128]{0:T(256)(128)(2,1)S(1)}, bf16[128]{0:T(256)(128)(2,1)}, u32[]{:S(2)}) copy-start(bf16[128]{0:T(256)(128)(2,1)} %param.29) | copy-start | bytes 772
  443.9 369.9 %copy-start.38 = (u32[128]{0:T(128)S(1)}, u32[128]{0:T(128)}, u32[]{:S(2)}) copy-start(u32[128]{0:T(128)} %constant.64) | copy-start | bytes 1540
  443.9 371.8 %copy-start.11 = (f32[16,64,320]{2,1,0:T(8,128)S(1)}, f32[16,64,320]{2,1,0:T(8,128)}, u32[]{:S(2)}) copy-start(f32[16,64,320]{2,1,0:T(8,128)} %get-tuple-element.57) | copy-start | bytes 3932164
  443.9 475.8 %all-reduce.14.cloned.1.call-start = ((), (), s32[]{:S(2)}) async-start(), calls=%async_computation.13 | async-start | bytes 4718592 | tf_op jit(solution)/shard_map/psum | solution.py:339
  693.5 122.6 %copy-start.8 = (bf16[320,1024]{1,0:T(8,128)(2,1)S(1)}, bf16[320,1024]{1,0:T(8,128)(2,1)}, u32[]{:S(2)}) copy-start(bf16[320,1024]{1,0:T(8,128)(2,1)} %param.15) | copy-start | bytes 1966084
  693.5 300.0 %all-gather.24.cloned.1.call-start = ((), (), s32[]{:S(2)}) async-start(), calls=%async_computation.12 | async-start | bytes 13369344 | tf_op jit(solution)/shard_map/all_gather | solution.py:336
  816.0 78.2 %copy-start.5 = (f32[320,1024]{1,0:T(8,128)S(1)}, f32[320,1024]{1,0:T(8,128)}, u32[]{:S(2)}) copy-start(f32[320,1024]{1,0:T(8,128)} %copy-done.4) | copy-start | bytes 3932164
  823.7 73.4 %copy-start.3 = (f32[320,1024]{1,0:T(8,128)S(1)}, f32[320,1024]{1,0:T(8,128)}, u32[]{:S(2)}) copy-start(f32[320,1024]{1,0:T(8,128)} %copy-done.2) | copy-start | bytes 3932164
  919.7 4.7 copy-start.18
  (4 other events, 6.1 us)
Sparse Core Ops, SparseCore 0:
  10.4 91.6 all-gather.15
  104.5 51.9 all-gather.17
  158.9 104.9 all-gather.19
  266.1 104.9 all-gather.21
  386.7 72.8 reduce-scatter.6
  463.3 112.8 reduce-scatter.8
  580.5 112.9 reduce-scatter.10
  697.3 96.4 reduce-scatter.4
  796.5 123.1 all-reduce.13
  921.2 72.2 all-gather.23
